TPU v7x, 256 devices: a whole 4x4x8 slice. The times are simulated.
256 devices in a mesh: seq: 32 (over y, z_lo, core), head: 8 (over x, z_hi).
Axes of the slice: x: 4, y: 4, z: 8 (z_hi: 2, z_lo: 4; z = z_hi * 4 + z_lo), core: 2. Of those that a mesh axis runs over, the one named last changes fastest.
Arguments:
- queries: bfloat16 [4096, 8192], P('seq', 'head'), may hold values from -48 to 48
- keyval: bfloat16 [4096, 2048], P('seq', 'head'), may hold values from -48 to 48
- grad_out: bfloat16 [4096, 8192], P('seq', 'head'), may hold values from -6 to 6
- doc_ids: int32 [4096], P('seq'), may hold values from 0 to 3, never falling along the last dimension, each value on 1 to 2048 neighbouring positions
- deltas: bfloat16 [8, 4096, 8192], P('head', 'seq'), may hold values from -6 to 6
- node_weights: bfloat16 [8192, 2048], P('head', 'seq'), may hold values from -0.0625 to 0.0625
- layer_slot: int32 [8], replicated, may hold values from 0 to 7, each once
Outputs:
- grad_query: bfloat16 [4096, 8192], P('seq', 'head')
- grad_keyval: bfloat16 [4096, 2048], P('seq', 'head')
- scores: float32 [8, 16], replicated
Inputs may be any that keep to these rules, and one draw needn't show every extreme that they name: `layer_slot`: each of the 8 layers stands in exactly one slot. `doc_ids`: never falling along the sequence.
All inputs are finite; a program needn't handle non-finite values.
Results may differ from a plain program's by a relative error of at most 0.013.
Values may be sent and summed in bfloat16 or wider, within the bound.
A program may use at most 64 MiB of HBM per device.

v0:
```python
import math
import jax
import jax.numpy as jnp
from jax import lax
from jax.sharding import PartitionSpec as P

H = 64
KVH = 8
HD = 128


def over_blocks(step, carry, pieces):
    total_rows = pieces[0].shape[0]
    block_rows = 512

    def one_turn(turn_index, running):
        offset = turn_index * block_rows
        blocks = tuple((lax.dynamic_slice_in_dim(piece, offset, block_rows, 0) for piece in pieces))
        return step(running, *blocks, offset)

    return lax.fori_loop(0, total_rows // block_rows, one_turn, carry)


def on_device(queries, keyval, grad_out, doc_ids, deltas, node_weights, layer_slot):
    tok_rows = queries.shape[0]
    kv_local = keyval.shape[1] // (2 * HD)
    group_size = H // KVH
    score_scale = 1.0 / math.sqrt(HD)
    seq_total = tok_rows * lax.axis_size("seq")
    query_grid = queries.reshape(tok_rows, kv_local, group_size, HD)
    out_grid = grad_out.reshape(tok_rows, kv_local, group_size, HD)
    row_positions = lax.axis_index("seq") * tok_rows + jnp.arange(tok_rows, dtype=jnp.int32)

    def block_logits(kv_rows, key_ids, key_start):
        width = kv_rows.shape[0]
        kv_grid = kv_rows.reshape(width, kv_local, 2, HD)
        logits = (
            jnp.einsum(
                "tgie,rge->gitr", query_grid, kv_grid[:, :, 0], preferred_element_type=jnp.float32
            )
            * score_scale
        )
        key_positions = key_start + jnp.arange(width, dtype=jnp.int32)
        allowed = (key_ids[None, :] == doc_ids[:, None]) & (
            key_positions[None, :] <= row_positions[:, None]
        )
        return (logits, allowed, kv_grid)

    def forward_step(carry, kv_rows, key_ids, key_start):
        run_max, run_sum, accum = carry
        logits, allowed, kv_grid = block_logits(kv_rows, key_ids, key_start)
        new_max = jnp.maximum(run_max, jnp.max(jnp.where(allowed, logits, -1e30), axis=3))
        weights = jnp.where(allowed, jnp.exp(logits - new_max[..., None]), 0.0)
        factor = jnp.exp(run_max - new_max)
        run_sum = run_sum * factor + jnp.sum(weights, axis=3)
        values = kv_grid[:, :, 1].astype(jnp.float32)
        accum = accum * factor[..., None] + jnp.einsum(
            "gitr,rge->gite", weights, values, precision=lax.Precision.HIGHEST
        )
        return (new_max, run_sum, accum)

    stat_shape = (kv_local, group_size, tok_rows)
    forward_init = (
        jnp.full(stat_shape, -1e30, jnp.float32),
        jnp.zeros(stat_shape, jnp.float32),
        jnp.zeros(stat_shape + (HD,), jnp.float32),
    )
    run_max, run_sum, accum = over_blocks(
        forward_step,
        forward_init,
        (
            lax.all_gather(keyval, "seq", axis=0, tiled=True),
            lax.all_gather(doc_ids, "seq", axis=0, tiled=True),
        ),
    )
    log_total = run_max + jnp.log(run_sum)
    attn_out = accum / run_sum[..., None]
    row_dot = jnp.einsum(
        "tgie,gite->git", out_grid.astype(jnp.float32), attn_out, precision=lax.Precision.HIGHEST
    )

    def backward_step(carry, kv_rows, key_ids, key_start):
        query_accum = carry[0]
        width = kv_rows.shape[0]
        logits, allowed, kv_grid = block_logits(kv_rows, key_ids, key_start)
        probs = jnp.where(allowed, jnp.exp(logits - log_total[..., None]), 0.0)
        grad_probs = jnp.einsum(
            "tgie,rge->gitr", out_grid, kv_grid[:, :, 1], preferred_element_type=jnp.float32
        )
        grad_logits = (probs * (grad_probs - row_dot[..., None])).astype(jnp.bfloat16)
        query_accum = (
            query_accum
            + jnp.einsum(
                "gitr,rge->gite", grad_logits, kv_grid[:, :, 0], preferred_element_type=jnp.float32
            )
            * score_scale
        )
        probs_low = probs.astype(jnp.bfloat16)
        grad_keys = (
            jnp.einsum(
                "gitr,tgie->rge", grad_logits, query_grid, preferred_element_type=jnp.float32
            )
            * score_scale
        )
        grad_values = jnp.einsum(
            "gitr,tgie->rge", probs_low, out_grid, preferred_element_type=jnp.float32
        )
        block_grad = jnp.stack((grad_keys, grad_values), axis=2).reshape(width, kv_local * 2 * HD)
        kv_buffer = lax.dynamic_update_slice(
            carry[1], block_grad, (key_start, jnp.zeros((), jnp.int32))
        )
        return (query_accum, kv_buffer)

    query_zero = jnp.zeros(stat_shape + (HD,), jnp.float32)
    backward_init = (query_zero, jnp.zeros((seq_total, kv_local * 2 * HD), jnp.float32))
    backward_out = over_blocks(
        backward_step,
        backward_init,
        (
            lax.all_gather(keyval, "seq", axis=0, tiled=True),
            lax.all_gather(doc_ids, "seq", axis=0, tiled=True),
        ),
    )
    query_accum = backward_out[0]
    grad_query = (
        jnp.transpose(query_accum, (2, 0, 1, 3))
        .reshape(tok_rows, kv_local * group_size * HD)
        .astype(jnp.bfloat16)
    )
    grad_keyval = lax.psum_scatter(
        backward_out[1].astype(jnp.bfloat16), "seq", scatter_dimension=0, tiled=True
    )
    width_deltas = lax.all_to_all(deltas, "head", split_axis=2, concat_axis=0, tiled=True)
    grad_rows = lax.all_gather(grad_keyval, "head", axis=1, tiled=True)
    layer_count = width_deltas.shape[0]
    node_count = grad_rows.shape[1] // HD
    projected = jnp.einsum(
        "ltd,dc->ltc",
        width_deltas,
        lax.all_gather(node_weights, "seq", axis=1, tiled=True),
        preferred_element_type=jnp.float32,
    )
    grad_cols = grad_rows.astype(jnp.float32)
    per_column = jnp.sum(projected * grad_cols[None], axis=1)
    partial_value = jnp.sum(per_column.reshape(layer_count, node_count, HD), axis=2)
    totals = lax.psum(partial_value / math.sqrt(seq_total), ("seq", "head"))
    placing = (layer_slot[:, None] == jnp.arange(layer_count, dtype=jnp.int32)[None, :]).astype(
        jnp.float32
    )
    scores = jnp.dot(placing.T, totals, precision=lax.Precision.HIGHEST)
    return (grad_query, grad_keyval, scores)


def solution(mesh):
    return jax.shard_map(
        on_device,
        mesh=mesh,
        in_specs=(
            P("seq", "head"),
            P("seq", "head"),
            P("seq", "head"),
            P("seq"),
            P("head", "seq", None),
            P("head", "seq"),
            P(),
        ),
        out_specs=(P("seq", "head"), P("seq", "head"), P()),
        check_vma=False,
    )
```

profile of v0, /device:TPU:1, one launch (start us, length us, event | category | flops | bytes accessed | tf_op | source)
XLA Modules:
  0.0 491.0 jit_solution(3479772316284741002)
XLA Ops:
  7.2 1.6 copy.67
  8.9 1.1 copy.68
  10.0 0.9 copy.69
  10.9 1.1 copy.70
  12.0 1.7 copy.96
  13.7 46.0 %all-gather = s32[32,1,128]{2,1,0:T(1,128)S(1)} all-gather(s32[1,1,128]{2,1,0:T(1,128)S(1)} %bitcast.262), channel_id=1, replica_groups=mesh['seq'=32,'head'=8] {'seq'}, dimensions={0}, use_global_device_ids=true | all-gather | bytes 16896 | tf_op jit(solution)/shard_map/all_gather | solution.py:121
  59.7 18.1 %all-gather.4.cloned.1.call-done = bf16[4096,256]{0,1:T(8,128)(2,1)} async-done(((bf16[128,256]{0,1:T(8,128)(2,1)}), bf16[4096,256]{0,1:T(8,128)(2,1)}) %all-gather.4.cloned.1.call-update) | async-done | bytes 2097168 | tf_op jit(solution)/shard_map/all_gather | solution.py:120
  77.8 55.1 %while.34 = (s32[]{:T(128)}, f32[1,8,128]{2,1,0:T(8,128)S(1)}, f32[1,8,128]{2,1,0:T(8,128)S(1)}, f32[1,8,128,128]{3,2,1,0:T(8,128)}, s32[4096]{0:T(1024)S(1)}, /...) while((s32[]{:T(128)}, f32[1,8,128]{2,1,0:T(8,128)S(1)}, ...), condition=%wide.region_3.4_spmd.clone, body=%wide.region_0.3_spmd.clone.sunk | while | flops 945363584 | bytes 8728263 | solution.py:21
  78.1 1.0 constant_dynamic-slice_fusion.4
  79.1 1.4 fusion.67
  80.6 2.8 fusion.70
  84.1 1.0 constant_dynamic-slice_fusion.4
  85.1 1.4 fusion.67
  86.6 3.8 fusion.70
  91.1 1.0 constant_dynamic-slice_fusion.4
  92.1 1.4 fusion.67
  93.6 3.8 fusion.70
  98.2 1.0 constant_dynamic-slice_fusion.4
  99.1 1.4 fusion.67
  100.6 3.8 fusion.70
  105.2 1.0 constant_dynamic-slice_fusion.4
  106.2 1.4 fusion.67
  107.6 3.8 fusion.70
  112.2 1.0 constant_dynamic-slice_fusion.4
  113.2 1.4 fusion.67
  114.6 3.8 fusion.70
  119.2 1.0 constant_dynamic-slice_fusion.4
  120.2 1.4 fusion.67
  121.7 3.8 fusion.70
  126.2 1.0 constant_dynamic-slice_fusion.4
  127.2 1.4 fusion.67
  128.7 3.8 fusion.70
  133.0 1.2 divide_bitcast_fusion
  134.2 1.3 multiply_reduce_fusion.1
  135.6 1.6 broadcast_in_dim.87.clone
  137.2 39.6 %while.35 = (s32[]{:T(128)}, f32[1,8,128,128]{3,2,1,0:T(8,128)S(1)}, bf16[4096,256]{1,0:T(8,128)(2,1)}, s32[4096]{0:T(1024)S(1)}, s32[128]{0:T(128)S(1)}, /*inde...) while((s32[]{:T(128)}, ...), condition=%wide.region_5.6_spmd.clone, body=%wide.region_4.5_spmd.clone.sunk | while | flops 675611264 | bytes 14438105 | solution.py:21
  137.5 1.0 constant_dynamic-slice_fusion.5
  142.4 1.0 constant_dynamic-slice_fusion.5
  147.3 1.0 constant_dynamic-slice_fusion.5
  150.6 0.7 constant_dynamic-update-slice_fusion.2
  152.3 1.0 constant_dynamic-slice_fusion.5
  155.5 0.7 constant_dynamic-update-slice_fusion.2
  157.3 1.0 constant_dynamic-slice_fusion.5
  162.2 1.0 constant_dynamic-slice_fusion.5
  165.4 0.7 constant_dynamic-update-slice_fusion.2
  167.2 1.0 constant_dynamic-slice_fusion.5
  170.4 0.7 constant_dynamic-update-slice_fusion.2
  172.1 1.0 constant_dynamic-slice_fusion.5
  177.5 0.8 copy-done
  178.3 6.9 %copy.73 = bf16[1,128,8192]{1,0,2:T(2,128)(2,1)} copy(bf16[1,128,8192]{2,1,0:T(8,128)(2,1)S(1)} %copy-done) | data formatting | bytes 4194304 | tf_op args[4]
  185.7 45.2 %reduce.8 = bf16[8192,128]{1,0:T(8,128)(2,1)S(1)} reduce(bf16[8192,1,128]{2,1,0:T(2,128)(2,1)} %bitcast.245, bf16[]{:T(256)} %broadcast.122), dimensions={1}, to_apply=%bitcast.163.reduce_sub_computation | reduce | bytes 4194306
  230.9 3.2 reshape.216
  234.1 54.8 %all_to_all.18 = bf16[8,2,65536]{2,1,0:T(2,128)(2,1)S(1)} all-to-all(bf16[8,2,65536]{2,1,0:T(2,128)(2,1)} %reshape.216), channel_id=1, replica_groups=mesh['seq'=32,'head'=8] {'head'}, dimensions={0} | all-to-all | bytes 4194304 | tf_op jit(solution)/shard_map/all_to_all | solution.py:133
  288.9 4.4 reshape.217
  293.3 2.5 copy.93
  295.8 2.6 copy.74
  298.6 0.8 copy.100
  299.4 31.5 %reduce-scatter.2.cloned.1.call-done = bf16[128,256]{1,0:T(8,128)(2,1)} async-done(((bf16[4096,256]{1,0:T(8,128)(2,1)}), bf16[128,256]{1,0:T(8,128)(2,1)}) %reduce-scatter.2.cloned.1.call-update) | async-done | bytes 65552 | tf_op jit(solution)/shard_map/reduce_scatter | solution.py:130
  330.9 42.4 %all_gather.17 = bf16[128,2048]{1,0:T(8,128)(2,1)S(1)} all-gather(bf16[128,256]{1,0:T(8,128)(2,1)} %reduce-scatter.2.cloned.1.call-done), channel_id=1, replica_groups=mesh['seq'=32,'head'=8] {'head'}, dimensions={1}, use_global_device_ids=true | all-gather | bytes 589824 | tf_op jit(solution)/shard_map/all_gather | solution.py:134
  373.3 1.1 convert_element_type.38
  374.4 26.8 %all-gather.6.cloned.1.call-done = bf16[1024,2048]{0,1:T(8,128)(2,1)} async-done(((bf16[1024,64]{0,1:T(8,128)(2,1)}), bf16[1024,2048]{0,1:T(8,128)(2,1)}) %all-gather.6.cloned.1.call-update) | async-done | bytes 4194320 | tf_op jit(solution)/shard_map/all_gather | solution.py:140
  401.1 7.2 %multiply_reduce_fusion = f32[8,2048]{1,0:T(8,128)S(1)} fusion(bf16[1024,2048]{0,1:T(8,128)(2,1)} %all-gather.6.cloned.1.call-done, f32[128,2048]{1,0:T(8,128)} %convert_element_type.38, bf16[1,128,8,1024]{3,1,2,0:T(8,128)(2,1)S(1)} %copy-done.1), kind=kOutput, calls=%fused_computation.60 | convolution fusion | flops 4299145216 | bytes 7405568 | tf_op jit(solution)/shard_map/ltd,dc->ltc/dot_general | solution.py:137
  408.4 75.2 %psum.7 = f32[8,16]{0,1:T(8,128)S(1)} all-reduce(f32[8,16]{0,1:T(8,128)S(1)} %broadcast_multiply_fusion), channel_id=1, replica_groups=mesh['seq'=32,'head'=8] {'seq','head'}, use_global_device_ids=true, to_apply=%region_9.10 | all-reduce | flops 128 | bytes 1024 | tf_op jit(solution)/shard_map/psum | solution.py:146
  483.6 0.8 fusion.44
  (180 shorter events, 35.8 us)
Async XLA Ops:
  7.2 6.6 %copy-start.2 = (s32[128]{0:T(128)S(1)}, s32[128]{0:T(128)}, u32[]{:S(2)}) copy-start(s32[128]{0:T(128)} %param.14) | copy-start | bytes 1540
  7.2 70.7 %all-gather.4.cloned.1.call-start = ((), (), s32[]{:S(2)}) async-start(), calls=%async_computation.2 | async-start | bytes 2162688 | tf_op jit(solution)/shard_map/all_gather | solution.py:120
  8.8 322.0 %reduce-scatter.2.cloned.1.call-start = ((), (), s32[]{:S(2)}) async-start(), calls=%async_computation.3 | async-start | bytes 2162688 | tf_op jit(solution)/shard_map/reduce_scatter | solution.py:130
  176.8 1.6 copy-start
  176.8 224.4 %all-gather.6.cloned.1.call-start = ((), (), s32[]{:S(2)}) async-start(), calls=%async_computation.4 | async-start | bytes 4325376 | tf_op jit(solution)/shard_map/all_gather | solution.py:140
  298.4 102.7 %copy-start.1 = (bf16[1,128,8,1024]{3,1,2,0:T(8,128)(2,1)S(1)}, bf16[1,128,8,1024]{3,1,2,0:T(8,128)(2,1)}, u32[]{:S(2)}) copy-start(bf16[1,128,8,1024]{3,1,2,0:T(8,128)(2,1)} %copy.74) | copy-start | bytes 6291460
  374.4 109.2 %copy-start.3 = (s32[8]{0:T(128)S(1)}, s32[8]{0:T(128)}, u32[]{:S(2)}) copy-start(s32[8]{0:T(128)} %param.17) | copy-start | bytes 100
Sparse Core Ops, SparseCore 0:
  10.3 67.4 all-gather.3
  176.9 153.8 reduce-scatter.1
  332.7 68.3 all-gather.5
where the time goes:
time: 493 us; the launch traced here: 491 us
  blocking collectives  218 us (44%)
  waiting for transfers between devices  76.9 us (16%)
  matrix products  70.4 us (14%)
  other arithmetic  56.2 us (11%)
  local copies, waits for them, and re-layouts  53.6 us (11%)
  between operations  13.9 us (3%)
    psum x1, blocking collectives, on_device(): totals = lax.psum(partial_value / math.sqrt(seq_total), ('seq', 'head'))  75.2 us
    all_to_all x1, blocking collectives, on_device(): lax.all_to_all(deltas, 'head', split_axis=2, concat_axis=0, tiled=True)  54.8 us
    unnamed x6, other arithmetic  46.5 us
    all_gather x1, blocking collectives, on_device(): lax.all_gather(doc_ids, 'seq', axis=0, tiled=True)  46 us
    all_gather x1, blocking collectives, on_device(): grad_rows = lax.all_gather(grad_keyval, 'head', axis=1, tiled=True)  42.4 us
    reduce_scatter x1, waiting for transfers between devices, on_device(): lax.psum_scatter(backward_out[1].astype(jnp.bfloat16), 'seq', scatter_dim...  31.5 us
    dot_general x8, matrix products, forward_step(): jnp.einsum('gitr,rge->gite', weights, values, precision=lax.Precision.HIG...  29.4 us
    all_gather x1, waiting for transfers between devices, on_device(): lax.all_gather(node_weights, 'seq', axis=1, tiled=True)  26.8 us
  transfers between devices with their start and end apart: 3, of which 3 were waited for; matrix products, arithmetic and copies ran while one was open for 15% of the time, Pallas kernels for 0%

commit v1 on v0

--- a/solution.py
+++ b/solution.py
@@ -143,7 +143,9 @@
     grad_cols = grad_rows.astype(jnp.float32)
     per_column = jnp.sum(projected * grad_cols[None], axis=1)
     partial_value = jnp.sum(per_column.reshape(layer_count, node_count, HD), axis=2)
-    totals = lax.psum(partial_value / math.sqrt(seq_total), ("seq", "head"))
+    totals = partial_value / math.sqrt(seq_total)
+    for h in ("seq", "head"):
+        totals = lax.psum(totals, axis_name=h)
     placing = (layer_slot[:, None] == jnp.arange(layer_count, dtype=jnp.int32)[None, :]).astype(
         jnp.float32
     )

time: 493 us -> 515 us (1.045)
  blocking collectives: 218 us -> 237 us
    psum x1 -> x2, blocking collectives: 75.2 us -> 93.6 us  [on_device(): totals = lax.psum(totals, axis_name=h)]
  transfers between devices with their start and end apart: 3 -> 3, of which waited for: 3 -> 3; matrix products, arithmetic and copies ran while one was open for 15% -> 14% of each run, Pallas kernels for 0% -> 0%
where the time goes in v1:
time: 515 us; the launch traced here: 509 us
  blocking collectives  237 us (46%)
  waiting for transfers between devices  76.9 us (15%)
  matrix products  70.4 us (14%)
  other arithmetic  56.2 us (11%)
  local copies, waits for them, and re-layouts  53.6 us (10%)
  between operations  13.9 us (3%)
    psum x2, blocking collectives, on_device(): totals = lax.psum(totals, axis_name=h)  93.6 us
    all_to_all x1, blocking collectives, on_device(): lax.all_to_all(deltas, 'head', split_axis=2, concat_axis=0, tiled=True)  54.8 us
    unnamed x6, other arithmetic  46.5 us
    all_gather x1, blocking collectives, on_device(): lax.all_gather(doc_ids, 'seq', axis=0, tiled=True)  46 us
    all_gather x1, blocking collectives, on_device(): grad_rows = lax.all_gather(grad_keyval, 'head', axis=1, tiled=True)  42.4 us
    reduce_scatter x1, waiting for transfers between devices, on_device(): lax.psum_scatter(backward_out[1].astype(jnp.bfloat16), 'seq', scatter_dim...  31.5 us
    dot_general x8, matrix products, forward_step(): jnp.einsum('gitr,rge->gite', weights, values, precision=lax.Precision.HIG...  29.4 us
    all_gather x1, waiting for transfers between devices, on_device(): lax.all_gather(node_weights, 'seq', axis=1, tiled=True)  26.8 us
  transfers between devices with their start and end apart: 3, of which 3 were waited for; matrix products, arithmetic and copies ran while one was open for 14% of the time, Pallas kernels for 0%

profile of v1, /device:TPU:1, one launch (start us, length us, event | category | flops | bytes accessed | tf_op | source)
XLA Modules:
  0.0 509.4 jit_solution(10893737290270238318)
XLA Ops:
  7.2 1.6 copy.67
  8.9 1.1 copy.68
  10.0 0.9 copy.69
  10.9 1.1 copy.70
  12.0 1.7 copy.96
  13.7 46.0 %all-gather = s32[32,1,128]{2,1,0:T(1,128)S(1)} all-gather(s32[1,1,128]{2,1,0:T(1,128)S(1)} %bitcast.262), channel_id=1, replica_groups=mesh['seq'=32,'head'=8] {'seq'}, dimensions={0}, use_global_device_ids=true | all-gather | bytes 16896 | tf_op jit(solution)/shard_map/all_gather | solution.py:121
  59.7 18.1 %all-gather.4.cloned.1.call-done = bf16[4096,256]{0,1:T(8,128)(2,1)} async-done(((bf16[128,256]{0,1:T(8,128)(2,1)}), bf16[4096,256]{0,1:T(8,128)(2,1)}) %all-gather.4.cloned.1.call-update) | async-done | bytes 2097168 | tf_op jit(solution)/shard_map/all_gather | solution.py:120
  77.8 55.1 %while.34 = (s32[]{:T(128)}, f32[1,8,128]{2,1,0:T(8,128)S(1)}, f32[1,8,128]{2,1,0:T(8,128)S(1)}, f32[1,8,128,128]{3,2,1,0:T(8,128)}, s32[4096]{0:T(1024)S(1)}, /...) while((s32[]{:T(128)}, f32[1,8,128]{2,1,0:T(8,128)S(1)}, ...), condition=%wide.region_3.4_spmd.clone, body=%wide.region_0.3_spmd.clone.sunk | while | flops 945363584 | bytes 8728263 | solution.py:21
  78.1 1.0 constant_dynamic-slice_fusion.4
  79.1 1.4 fusion.67
  80.6 2.8 fusion.70
  84.1 1.0 constant_dynamic-slice_fusion.4
  85.1 1.4 fusion.67
  86.6 3.8 fusion.70
  91.1 1.0 constant_dynamic-slice_fusion.4
  92.1 1.4 fusion.67
  93.6 3.8 fusion.70
  98.2 1.0 constant_dynamic-slice_fusion.4
  99.1 1.4 fusion.67
  100.6 3.8 fusion.70
  105.2 1.0 constant_dynamic-slice_fusion.4
  106.2 1.4 fusion.67
  107.6 3.8 fusion.70
  112.2 1.0 constant_dynamic-slice_fusion.4
  113.2 1.4 fusion.67
  114.6 3.8 fusion.70
  119.2 1.0 constant_dynamic-slice_fusion.4
  120.2 1.4 fusion.67
  121.7 3.8 fusion.70
  126.2 1.0 constant_dynamic-slice_fusion.4
  127.2 1.4 fusion.67
  128.7 3.8 fusion.70
  133.0 1.2 divide_bitcast_fusion
  134.2 1.3 multiply_reduce_fusion.1
  135.6 1.6 broadcast_in_dim.87.clone
  137.2 39.6 %while.35 = (s32[]{:T(128)}, f32[1,8,128,128]{3,2,1,0:T(8,128)S(1)}, bf16[4096,256]{1,0:T(8,128)(2,1)}, s32[4096]{0:T(1024)S(1)}, s32[128]{0:T(128)S(1)}, /*inde...) while((s32[]{:T(128)}, ...), condition=%wide.region_5.6_spmd.clone, body=%wide.region_4.5_spmd.clone.sunk | while | flops 675611264 | bytes 14438105 | solution.py:21
  137.5 1.0 constant_dynamic-slice_fusion.5
  142.4 1.0 constant_dynamic-slice_fusion.5
  147.3 1.0 constant_dynamic-slice_fusion.5
  150.6 0.7 constant_dynamic-update-slice_fusion.2
  152.3 1.0 constant_dynamic-slice_fusion.5
  155.5 0.7 constant_dynamic-update-slice_fusion.2
  157.3 1.0 constant_dynamic-slice_fusion.5
  162.2 1.0 constant_dynamic-slice_fusion.5
  165.4 0.7 constant_dynamic-update-slice_fusion.2
  167.2 1.0 constant_dynamic-slice_fusion.5
  172.1 1.0 constant_dynamic-slice_fusion.5
  177.5 0.8 copy-done
  178.3 6.9 %copy.73 = bf16[1,128,8192]{1,0,2:T(2,128)(2,1)} copy(bf16[1,128,8192]{2,1,0:T(8,128)(2,1)S(1)} %copy-done) | data formatting | bytes 4194304 | tf_op args[4]
  185.7 45.2 %reduce.8 = bf16[8192,128]{1,0:T(8,128)(2,1)S(1)} reduce(bf16[8192,1,128]{2,1,0:T(2,128)(2,1)} %bitcast.245, bf16[]{:T(256)} %broadcast.122), dimensions={1}, to_apply=%bitcast.163.reduce_sub_computation | reduce | bytes 4194306
  230.9 3.2 reshape.216
  234.1 54.8 %all_to_all.18 = bf16[8,2,65536]{2,1,0:T(2,128)(2,1)S(1)} all-to-all(bf16[8,2,65536]{2,1,0:T(2,128)(2,1)} %reshape.216), channel_id=1, replica_groups=mesh['seq'=32,'head'=8] {'head'}, dimensions={0} | all-to-all | bytes 4194304 | tf_op jit(solution)/shard_map/all_to_all | solution.py:133
  288.9 4.4 reshape.217
  293.3 2.5 copy.93
  295.8 2.6 copy.74
  298.6 0.8 copy.100
  299.4 31.5 %reduce-scatter.2.cloned.1.call-done = bf16[128,256]{1,0:T(8,128)(2,1)} async-done(((bf16[4096,256]{1,0:T(8,128)(2,1)}), bf16[128,256]{1,0:T(8,128)(2,1)}) %reduce-scatter.2.cloned.1.call-update) | async-done | bytes 65552 | tf_op jit(solution)/shard_map/reduce_scatter | solution.py:130
  330.9 42.4 %all_gather.17 = bf16[128,2048]{1,0:T(8,128)(2,1)S(1)} all-gather(bf16[128,256]{1,0:T(8,128)(2,1)} %reduce-scatter.2.cloned.1.call-done), channel_id=1, replica_groups=mesh['seq'=32,'head'=8] {'head'}, dimensions={1}, use_global_device_ids=true | all-gather | bytes 589824 | tf_op jit(solution)/shard_map/all_gather | solution.py:134
  373.3 1.1 convert_element_type.38
  374.4 26.8 %all-gather.6.cloned.1.call-done = bf16[1024,2048]{0,1:T(8,128)(2,1)} async-done(((bf16[1024,64]{0,1:T(8,128)(2,1)}), bf16[1024,2048]{0,1:T(8,128)(2,1)}) %all-gather.6.cloned.1.call-update) | async-done | bytes 4194320 | tf_op jit(solution)/shard_map/all_gather | solution.py:140
  401.1 7.2 %multiply_reduce_fusion = f32[8,2048]{1,0:T(8,128)S(1)} fusion(bf16[1024,2048]{0,1:T(8,128)(2,1)} %all-gather.6.cloned.1.call-done, f32[128,2048]{1,0:T(8,128)} %convert_element_type.38, bf16[1,128,8,1024]{3,1,2,0:T(8,128)(2,1)S(1)} %copy-done.1), kind=kOutput, calls=%fused_computation.60 | convolution fusion | flops 4299145216 | bytes 7405568 | tf_op jit(solution)/shard_map/ltd,dc->ltc/dot_general | solution.py:137
  408.4 68.0 %psum.14 = f32[8,16]{0,1:T(8,128)S(1)} all-reduce(f32[8,16]{0,1:T(8,128)S(1)} %broadcast_multiply_fusion), channel_id=1, replica_groups=mesh['seq'=32,'head'=8] {'seq'}, use_global_device_ids=true, to_apply=%region_9.10 | all-reduce | flops 128 | bytes 1024 | tf_op jit(solution)/shard_map/psum | solution.py:148
  476.4 25.6 %psum.15 = f32[8,16]{0,1:T(8,128)S(1)} all-reduce(f32[8,16]{0,1:T(8,128)S(1)} %psum.14), channel_id=1, replica_groups=mesh['seq'=32,'head'=8] {'head'}, use_global_device_ids=true, to_apply=%region_10.11 | all-reduce | flops 128 | bytes 1024 | tf_op jit(solution)/shard_map/psum | solution.py:148
  502.1 0.8 fusion.44
  (181 shorter events, 36.6 us)
Async XLA Ops:
  7.2 6.6 %copy-start.2 = (s32[128]{0:T(128)S(1)}, s32[128]{0:T(128)}, u32[]{:S(2)}) copy-start(s32[128]{0:T(128)} %param.14) | copy-start | bytes 1540
  7.2 70.7 %all-gather.4.cloned.1.call-start = ((), (), s32[]{:S(2)}) async-start(), calls=%async_computation.2 | async-start | bytes 2162688 | tf_op jit(solution)/shard_map/all_gather | solution.py:120
  8.8 322.0 %reduce-scatter.2.cloned.1.call-start = ((), (), s32[]{:S(2)}) async-start(), calls=%async_computation.3 | async-start | bytes 2162688 | tf_op jit(solution)/shard_map/reduce_scatter | solution.py:130
  176.8 1.6 copy-start
  176.8 224.4 %all-gather.6.cloned.1.call-start = ((), (), s32[]{:S(2)}) async-start(), calls=%async_computation.4 | async-start | bytes 4325376 | tf_op jit(solution)/shard_map/all_gather | solution.py:140
  298.4 102.7 %copy-start.1 = (bf16[1,128,8,1024]{3,1,2,0:T(8,128)(2,1)S(1)}, bf16[1,128,8,1024]{3,1,2,0:T(8,128)(2,1)}, u32[]{:S(2)}) copy-start(bf16[1,128,8,1024]{3,1,2,0:T(8,128)(2,1)} %copy.74) | copy-start | bytes 6291460
  374.4 127.7 %copy-start.3 = (s32[8]{0:T(128)S(1)}, s32[8]{0:T(128)}, u32[]{:S(2)}) copy-start(s32[8]{0:T(128)} %param.17) | copy-start | bytes 100
Sparse Core Ops, SparseCore 0:
  10.3 67.4 all-gather.3
  176.9 153.8 reduce-scatter.1
  332.7 68.3 all-gather.5
